TPU v7x, 128 devices: a whole 4x4x4 slice. The times are simulated.
128 devices in a mesh: mode: 16 (over z_hi, y, core), gx: 2 (over z_lo), gy: 4 (over x).
Axes of the slice: x: 4, y: 4, z: 4 (z_hi: 2, z_lo: 2; z = z_hi * 2 + z_lo), core: 2. Of those that a mesh axis runs over, the one named last changes fastest.
Arguments:
- right_side: float32 [16, 32, 28672], P('gx', 'gy', 'mode'), may hold values from -6 to 6
- col_block: int32 [224, 32], P('mode'), may hold values from 0 to 223, as said below
- blocks: bfloat16 [224, 32, 128, 128], P('mode'), may hold values from -0.09375 to 0.09375
- relax_rate: float32 [28672], P('mode'), may hold values from 0.5 to 4
- drift_speed: float32 [2, 28672], P(None, 'mode'), may hold values from 0.3 to 1.5
- upwind_sign: int32 [2, 28672], P(None, 'mode'), may hold values from 0 to 1
- wall_mask: int32 [16, 32], P('gx', 'gy'), may hold values 0 or 1
Outputs:
- solution: float32 [16, 32, 28672], P('gx', 'gy', 'mode')
- hessenberg: float32 [4, 3], replicated
Inputs may be any that keep to these rules, and one draw needn't show every extreme that they name: `col_block`: for every block row and every o in 0 .. 15, slots o * 2 to (o + 1) * 2 - 1 hold distinct column blocks of o * 14 to (o + 1) * 14 - 1.
All inputs are finite; a program needn't handle non-finite values. No bound on the sum of `wall_mask` on one device may be relied on, other than what follows from the above.
Results may differ from a plain program's by a relative error of at most 0.00081.
Values may be sent and summed in bfloat16 or wider, within the bound.
A program may use at most 128 MiB of HBM per device.

v0:
```python
import jax
import jax.numpy as jnp
from jax import lax
from jax.sharding import PartitionSpec as P

KRYLOV = 3


epsilon = 1e-12


def extended(block, sides, width):
    for axis, dim in sides:
        count = lax.axis_size(axis)
        forward = [(i, i + 1) for i in range(count - 1)]
        backward = [(target, source) for source, target in forward]
        low = lax.ppermute(
            lax.slice_in_dim(block, block.shape[dim] - width, None, axis=dim), axis, forward
        )
        high = lax.ppermute(lax.slice_in_dim(block, 0, width, axis=dim), axis, backward)
        block = jnp.concatenate([low, block, high], axis=dim)
    return block


def apply_operator(current, col_block, blocks, relax_rate, drift_speed, upwind_sign, open_cells):
    cells_first, cells_second, local_modes = current.shape
    block_size = blocks.shape[2]
    local_blocks = col_block.shape[0]
    slot_count = col_block.shape[1]
    masked = current * open_cells[:, :, None]
    padded = extended(masked, (("gx", 0), ("gy", 1)), 1)
    from_west = padded[:-2, 1:-1]
    from_east = padded[2:, 1:-1]
    from_south = padded[1:-1, :-2]
    from_north = padded[1:-1, 2:]
    upstream_first = jnp.where(upwind_sign[0] == 1, from_west, from_east)
    upstream_second = jnp.where(upwind_sign[1] == 1, from_south, from_north)
    drift_term = drift_speed[0] * (current - upstream_first) + drift_speed[1] * (
        current - upstream_second
    )
    cell_count = cells_first * cells_second
    rounded = current.astype(jnp.bfloat16).reshape(cell_count, local_modes)
    gathered = lax.all_gather(rounded, "mode", axis=1, tiled=True)
    gathered = gathered.reshape(cell_count, -1, block_size)
    picked = jnp.take(gathered, col_block.reshape(-1), axis=1)
    picked = picked.reshape(cell_count, local_blocks, slot_count, block_size)
    scattered = jnp.einsum("rsik,crsk->cri", blocks, picked, preferred_element_type=jnp.float32)
    scattered = scattered.reshape(cells_first, cells_second, local_modes)
    return relax_rate * current + drift_term - scattered


def least_squares(hessenberg, initial):
    upper = [
        [hessenberg[row_index, col_index] for col_index in range(KRYLOV)]
        for row_index in range(KRYLOV + 1)
    ]
    target = [initial] + [jnp.zeros_like(initial) for row_index in range(KRYLOV)]
    cosines = []
    sines = []
    for col_index in range(KRYLOV):
        for row_index in range(col_index):
            first = upper[row_index][col_index]
            second = upper[row_index + 1][col_index]
            upper[row_index][col_index] = cosines[row_index] * first + sines[row_index] * second
            upper[row_index + 1][col_index] = cosines[row_index] * second - sines[row_index] * first
        first = upper[col_index][col_index]
        second = upper[col_index + 1][col_index]
        radius = jnp.sqrt(first * first + second * second)
        cosine = first / radius
        sine_value = second / radius
        upper[col_index][col_index] = radius
        target[col_index + 1] = -sine_value * target[col_index]
        target[col_index] = cosine * target[col_index]
        cosines.append(cosine)
        sines.append(sine_value)
    combo = [None] * KRYLOV
    for row_index in reversed(range(KRYLOV)):
        running = target[row_index]
        for col_index in range(row_index + 1, KRYLOV):
            running = running - upper[row_index][col_index] * combo[col_index]
        combo[row_index] = running / upper[row_index][row_index]
    return combo


def per_device(right_side, col_block, blocks, relax_rate, drift_speed, upwind_sign, wall_mask):
    open_cells = (1 - wall_mask).astype(jnp.float32)
    squared = lax.psum(jnp.sum(right_side * right_side), ("mode", "gx", "gy"))
    initial = jnp.sqrt(squared + epsilon)
    krylov_basis = [right_side / initial]
    columns_list = []
    for section in range(KRYLOV):
        mapped = apply_operator(
            krylov_basis[section],
            col_block,
            blocks,
            relax_rate,
            drift_speed,
            upwind_sign,
            open_cells,
        )
        coefficients = []
        for earlier in range(section + 1):
            projection = lax.psum(jnp.sum(krylov_basis[earlier] * mapped), ("mode", "gx", "gy"))
            mapped = mapped - projection * krylov_basis[earlier]
            coefficients.append(projection)
        length = jnp.sqrt(lax.psum(jnp.sum(mapped * mapped), ("mode", "gx", "gy")) + epsilon)
        krylov_basis.append(mapped / length)
        entries = (
            coefficients
            + [length]
            + [jnp.zeros_like(length) for later in range(KRYLOV - section - 1)]
        )
        columns_list.append(jnp.stack(entries))
    hessenberg = jnp.stack(columns_list, axis=1)
    combo = least_squares(hessenberg, initial)
    solution = jnp.zeros_like(right_side)
    for section in range(KRYLOV):
        solution = solution + combo[section] * krylov_basis[section]
    return (solution, hessenberg)


def solution(mesh):
    return jax.shard_map(
        per_device,
        mesh=mesh,
        in_specs=(
            P("gx", "gy", "mode"),
            P("mode", None),
            P("mode", None, None, None),
            P("mode"),
            P(None, "mode"),
            P(None, "mode"),
            P("gx", "gy"),
        ),
        out_specs=(P("gx", "gy", "mode"), P()),
        check_vma=False,
    )
```

profile of v0, /device:TPU:0, one launch (start us, length us, event | category | flops | bytes accessed | tf_op | source)
XLA Modules:
  0.0 979.5 jit_solution(3949034539014777959)
XLA Ops:
  9.6 68.2 %psum.70 = f32[]{:T(128)} all-reduce(f32[]{:T(128)} %multiply_reduce_fusion.9), channel_id=1, replica_groups=mesh['mode'=16,'gx'=2,'gy'=4] {'mode','gx','gy'}, use_global_device_ids=true, to_apply=%region_1.0 | all-reduce | flops 1 | bytes 8 | tf_op jit(solution)/shard_map/psum | solution.py:87
  81.7 4.5 collective-permute-start
  90.2 4.5 collective-permute-start.2
  94.8 35.9 %all-gather.4.cloned.1.call-done = bf16[64,28672]{1,0:T(8,128)(2,1)} async-done(((bf16[64,1792]{1,0:T(8,128)(2,1)}), bf16[64,28672]{1,0:T(8,128)(2,1)}) %all-gather.4.cloned.1.call-update) | async-done | bytes 3670032 | tf_op jit(solution)/shard_map/all_gather | solution.py:43
  130.7 5.0 copy_bitcast_fusion.2
  135.7 21.7 %gather_fusion = bf16[448,64,128]{2,1,0:T(8,128)(2,1)} fusion(bf16[64,224,128]{2,0,1:T(8,128)(2,1)} %copy_bitcast_fusion.2, s32[1024]{0:T(1024)S(1)} %pad_clamp_fusion), kind=kCustom, calls=%fused_computation.clone | custom fusion | bytes 14681856 | tf_op jit(solution)/shard_map/jit(_take)/gather | solution.py:45
  157.4 7.0 broadcast_select_fusion.2
  164.4 12.4 %convolution_bitcast_fusion.2 = f32[64,14,128]{2,0,1:T(8,128)S(1)} fusion(bf16[64,14,32,128]{3,0,2,1:T(8,128)(2,1)} %bitcast.67, bf16[14,32,128,128]{3,2,1,0:T(8,128)(2,1)} %param.11), kind=kOutput, calls=%fused_computation.11 | convolution fusion | flops 939524096 | bytes 22478848 | tf_op jit(solution)/shard_map/rsik,crsk->cri/dot_general | solution.py:47
  178.1 64.9 %psum.71 = f32[]{:T(128)} all-reduce(f32[]{:T(128)} %get-tuple-element.23), channel_id=1, replica_groups=mesh['mode'=16,'gx'=2,'gy'=4] {'mode','gx','gy'}, use_global_device_ids=true, to_apply=%region_3.5 | all-reduce | flops 1 | bytes 8 | tf_op jit(solution)/shard_map/psum | solution.py:103
  244.4 64.1 %psum.72 = f32[]{:T(128)} all-reduce(f32[]{:T(128)} %multiply_reduce_fusion.7), channel_id=1, replica_groups=mesh['mode'=16,'gx'=2,'gy'=4] {'mode','gx','gy'}, use_global_device_ids=true, to_apply=%region_5.7 | all-reduce | flops 1 | bytes 8 | tf_op jit(solution)/shard_map/psum | solution.py:106
  312.0 4.5 collective-permute-start.4
  316.8 2.4 collective-permute-done.4
  320.5 4.5 collective-permute-start.6
  325.1 35.9 %all-gather.6.cloned.1.call-done = bf16[64,28672]{1,0:T(8,128)(2,1)} async-done(((bf16[64,1792]{1,0:T(8,128)(2,1)}), bf16[64,28672]{1,0:T(8,128)(2,1)}) %all-gather.6.cloned.1.call-update) | async-done | bytes 3670032 | tf_op jit(solution)/shard_map/all_gather | solution.py:43
  361.0 5.0 copy_bitcast_fusion.1
  366.0 21.7 %gather_fusion.1 = bf16[448,64,128]{2,1,0:T(8,128)(2,1)} fusion(bf16[64,224,128]{2,0,1:T(8,128)(2,1)} %copy_bitcast_fusion.1, s32[1024]{0:T(1024)S(1)} %pad_clamp_fusion), kind=kCustom, calls=%fused_computation.1.clone | custom fusion | bytes 14681856 | tf_op jit(solution)/shard_map/jit(_take)/gather | solution.py:45
  387.6 7.0 broadcast_select_fusion.1
  394.7 12.3 %convolution_bitcast_fusion.1 = f32[64,14,128]{2,0,1:T(8,128)S(1)} fusion(bf16[64,14,32,128]{3,0,2,1:T(8,128)(2,1)} %bitcast.68, bf16[14,32,128,128]{3,2,1,0:T(8,128)(2,1)} %param.11), kind=kOutput, calls=%fused_computation.10 | convolution fusion | flops 939524096 | bytes 22478848 | tf_op jit(solution)/shard_map/rsik,crsk->cri/dot_general | solution.py:47
  408.3 64.9 %psum.73 = f32[]{:T(128)} all-reduce(f32[]{:T(128)} %get-tuple-element.19), channel_id=1, replica_groups=mesh['mode'=16,'gx'=2,'gy'=4] {'mode','gx','gy'}, use_global_device_ids=true, to_apply=%region_7.9 | all-reduce | flops 1 | bytes 8 | tf_op jit(solution)/shard_map/psum | solution.py:103
  474.5 64.1 %psum.74 = f32[]{:T(128)} all-reduce(f32[]{:T(128)} %multiply_reduce_fusion.5), channel_id=1, replica_groups=mesh['mode'=16,'gx'=2,'gy'=4] {'mode','gx','gy'}, use_global_device_ids=true, to_apply=%region_9.11 | all-reduce | flops 1 | bytes 8 | tf_op jit(solution)/shard_map/psum | solution.py:103
  540.6 62.3 %psum.75 = f32[]{:T(128)} all-reduce(f32[]{:T(128)} %get-tuple-element.17), channel_id=1, replica_groups=mesh['mode'=16,'gx'=2,'gy'=4] {'mode','gx','gy'}, use_global_device_ids=true, to_apply=%region_11.13 | all-reduce | flops 1 | bytes 8 | tf_op jit(solution)/shard_map/psum | solution.py:106
  611.0 4.5 collective-permute-start.8
  618.8 4.5 collective-permute-start.10
  623.3 32.8 %all-gather.8.cloned.1.call-done = bf16[64,28672]{1,0:T(8,128)(2,1)} async-done(((bf16[64,1792]{1,0:T(8,128)(2,1)}), bf16[64,28672]{1,0:T(8,128)(2,1)}) %all-gather.8.cloned.1.call-update) | async-done | bytes 3670032 | tf_op jit(solution)/shard_map/all_gather | solution.py:43
  656.1 5.0 copy_bitcast_fusion
  661.1 21.7 %gather_fusion.2 = bf16[448,64,128]{2,1,0:T(8,128)(2,1)} fusion(bf16[64,224,128]{2,0,1:T(8,128)(2,1)} %copy_bitcast_fusion, s32[1024]{0:T(1024)S(1)} %pad_clamp_fusion), kind=kCustom, calls=%fused_computation.2.clone | custom fusion | bytes 14681856 | tf_op jit(solution)/shard_map/jit(_take)/gather | solution.py:45
  682.8 7.0 broadcast_select_fusion
  689.8 12.3 %convolution_bitcast_fusion = f32[64,14,128]{2,0,1:T(8,128)S(1)} fusion(bf16[64,14,32,128]{3,0,2,1:T(8,128)(2,1)} %bitcast.66, bf16[14,32,128,128]{3,2,1,0:T(8,128)(2,1)} %param.11), kind=kOutput, calls=%fused_computation.9 | convolution fusion | flops 939524096 | bytes 22478848 | tf_op jit(solution)/shard_map/rsik,crsk->cri/dot_general | solution.py:47
  703.5 64.9 %psum.76 = f32[]{:T(128)} all-reduce(f32[]{:T(128)} %get-tuple-element.15), channel_id=1, replica_groups=mesh['mode'=16,'gx'=2,'gy'=4] {'mode','gx','gy'}, use_global_device_ids=true, to_apply=%region_13.15 | all-reduce | flops 1 | bytes 8 | tf_op jit(solution)/shard_map/psum | solution.py:103
  769.8 64.1 %psum.77 = f32[]{:T(128)} all-reduce(f32[]{:T(128)} %multiply_reduce_fusion.2), channel_id=1, replica_groups=mesh['mode'=16,'gx'=2,'gy'=4] {'mode','gx','gy'}, use_global_device_ids=true, to_apply=%region_15.17 | all-reduce | flops 1 | bytes 8 | tf_op jit(solution)/shard_map/psum | solution.py:103
  837.3 62.3 %psum.78 = f32[]{:T(128)} all-reduce(f32[]{:T(128)} %get-tuple-element.13), channel_id=1, replica_groups=mesh['mode'=16,'gx'=2,'gy'=4] {'mode','gx','gy'}, use_global_device_ids=true, to_apply=%region_17.19 | all-reduce | flops 1 | bytes 8 | tf_op jit(solution)/shard_map/psum | solution.py:103
  903.4 64.7 %psum.79 = f32[]{:T(128)} all-reduce(f32[]{:T(128)} %multiply_reduce_fusion), channel_id=1, replica_groups=mesh['mode'=16,'gx'=2,'gy'=4] {'mode','gx','gy'}, use_global_device_ids=true, to_apply=%region_19.21 | all-reduce | flops 1 | bytes 8 | tf_op jit(solution)/shard_map/psum | solution.py:106
  (67 shorter events, 36.8 us)
Async XLA Ops:
  7.2 123.5 %all-gather.4.cloned.1.call-start = ((), (), s32[]{:S(2)}) async-start(), calls=%async_computation | async-start | bytes 3899392 | tf_op jit(solution)/shard_map/all_gather | solution.py:43
  80.3 280.6 %all-gather.6.cloned.1.call-start = ((), (), s32[]{:S(2)}) async-start(), calls=%async_computation.1 | async-start | bytes 3899392 | tf_op jit(solution)/shard_map/all_gather | solution.py:43
  80.4 8.4 collective-permute-start.1
  81.7 7.1 collective-permute-start
  88.9 88.2 %collective-permute-start.3 = (f32[10,1,1792]{2,1,0:T(1,128)S(1)}, f32[10,1,1792]{2,1,0:T(1,128)S(1)}, u32[]{:S(2)}, u32[]{:S(2)}) collective-permute-start(f32[10,1,1792]{2,1,0:T(1,128)S(1)} %get-tuple-element.30), channel_id=1, source_target_pairs={{1,0},{2,1},{3,2},{5,4},{6,5},{7,6},{9,8},{10,9},{11,10},{13,12},{... | collective-permute-start | bytes 215048 | tf_op jit(solution)/shard_map/ppermute | solution.py:20
  90.2 86.9 %collective-permute-start.2 = (f32[10,1,1792]{2,1,0:T(1,128)S(1)}, f32[10,1,1792]{2,1,0:T(1,128)S(1)}, u32[]{:S(2)}, u32[]{:S(2)}) collective-permute-start(f32[10,1,1792]{2,1,0:T(1,128)S(1)} %get-tuple-element.29), channel_id=1, source_target_pairs={{0,1},{1,2},{2,3},{4,5},{5,6},{6,7},{8,9},{9,10},{10,11},{12,13},{... | collective-permute-start | bytes 215048 | tf_op jit(solution)/shard_map/ppermute | solution.py:17
  164.4 12.8 %copy-start = (f32[8,8,1792]{2,1,0:T(8,128)S(1)}, f32[8,8,1792]{2,1,0:T(8,128)}, u32[]{:S(2)}) copy-start(f32[8,8,1792]{2,1,0:T(8,128)} %param.9) | copy-start | bytes 1376260
  164.4 12.8 %copy-start.1 = (f32[1792]{0:T(1024)S(1)}, f32[1792]{0:T(1024)}, u32[]{:S(2)}) copy-start(f32[1792]{0:T(1024)} %param.12) | copy-start | bytes 21508
  310.6 345.5 %all-gather.8.cloned.1.call-start = ((), (), s32[]{:S(2)}) async-start(), calls=%async_computation.2 | async-start | bytes 3899392 | tf_op jit(solution)/shard_map/all_gather | solution.py:43
  310.7 6.1 collective-permute-start.5
  312.0 7.1 collective-permute-start.4
  319.2 88.1 %collective-permute-start.7 = (f32[10,1,1792]{2,1,0:T(1,128)S(1)}, f32[10,1,1792]{2,1,0:T(1,128)S(1)}, u32[]{:S(2)}, u32[]{:S(2)}) collective-permute-start(f32[10,1,1792]{2,1,0:T(1,128)S(1)} %get-tuple-element.28), channel_id=1, source_target_pairs={{1,0},{2,1},{3,2},{5,4},{6,5},{7,6},{9,8},{10,9},{11,10},{13,12},{... | collective-permute-start | bytes 215048 | tf_op jit(solution)/shard_map/ppermute | solution.py:20
  320.5 86.9 %collective-permute-start.6 = (f32[10,1,1792]{2,1,0:T(1,128)S(1)}, f32[10,1,1792]{2,1,0:T(1,128)S(1)}, u32[]{:S(2)}, u32[]{:S(2)}) collective-permute-start(f32[10,1,1792]{2,1,0:T(1,128)S(1)} %get-tuple-element.27), channel_id=1, source_target_pairs={{0,1},{1,2},{2,3},{4,5},{5,6},{6,7},{8,9},{9,10},{10,11},{12,13},{... | collective-permute-start | bytes 215048 | tf_op jit(solution)/shard_map/ppermute | solution.py:17
  609.7 7.2 collective-permute-start.9
  611.0 6.4 collective-permute-start.8
  617.5 85.0 %collective-permute-start.11 = (f32[10,1,1792]{2,1,0:T(1,128)S(1)}, f32[10,1,1792]{2,1,0:T(1,128)S(1)}, u32[]{:S(2)}, u32[]{:S(2)}) collective-permute-start(f32[10,1,1792]{2,1,0:T(1,128)S(1)} %get-tuple-element.26), channel_id=1, source_target_pairs={{1,0},{2,1},{3,2},{5,4},{6,5},{7,6},{9,8},{10,9},{11,10},{13,12},{... | collective-permute-start | bytes 215048 | tf_op jit(solution)/shard_map/ppermute | solution.py:20
  618.8 83.7 %collective-permute-start.10 = (f32[10,1,1792]{2,1,0:T(1,128)S(1)}, f32[10,1,1792]{2,1,0:T(1,128)S(1)}, u32[]{:S(2)}, u32[]{:S(2)}) collective-permute-start(f32[10,1,1792]{2,1,0:T(1,128)S(1)} %get-tuple-element.25), channel_id=1, source_target_pairs={{0,1},{1,2},{2,3},{4,5},{5,6},{6,7},{8,9},{9,10},{10,11},{12,13},{... | collective-permute-start | bytes 215048 | tf_op jit(solution)/shard_map/ppermute | solution.py:17
Sparse Core Ops, SparseCore 0:
  80.4 50.1 all-gather.3
  310.7 50.1 all-gather.5
  604.4 51.6 all-gather.7
where the time goes:
time: 992 us; the launch traced here: 979 us
  blocking collectives  644 us (65%)
  waiting for transfers between devices  108 us (11%)
  local copies, waits for them, and re-layouts  83.4 us (8%)
  other arithmetic  45.7 us (5%)
  matrix products  37 us (4%)
  starting transfers between devices  35.2 us (4%)
  between operations  26 us (3%)
    psum x6, blocking collectives, per_device(): lax.psum(jnp.sum(krylov_basis[earlier] * mapped), ('mode', 'gx', 'gy'))  385 us
    psum x3, blocking collectives, per_device(): lax.psum(jnp.sum(mapped * mapped), ('mode', 'gx', 'gy')) + epsilon  191 us
    all_gather x3, waiting for transfers between devices, apply_operator(): gathered = lax.all_gather(rounded, 'mode', axis=1, tiled=True)  105 us
    psum x1, blocking collectives, per_device(): squared = lax.psum(jnp.sum(right_side * right_side), ('mode', 'gx', 'gy'))  68.2 us
    gather x3, local copies, waits for them, and re-layouts, apply_operator(): picked = jnp.take(gathered, col_block.reshape(-1), axis=1)  65 us
    dot_general x3, matrix products, apply_operator(): jnp.einsum('rsik,crsk->cri', blocks, picked, preferred_element_type=jnp.f...  37 us
    ppermute x6, starting transfers between devices, extended(): lax.ppermute(lax.slice_in_dim(block, block.shape[dim] - width, None, axis...  27.3 us
    select_n x4, other arithmetic, apply_operator(): picked = jnp.take(gathered, col_block.reshape(-1), axis=1)  21.1 us
  transfers between devices with their start and end apart: 15, of which 7 were waited for; matrix products, arithmetic and copies ran while one was open for 15% of the time, Pallas kernels for 0%

commit v1 on v0

v1 whole, which is shorter than its diff:
```python
import functools

import jax
import jax.numpy as jnp
from jax import lax
from jax.experimental import pallas as pl
from jax.experimental.pallas import tpu as pltpu
from jax.sharding import PartitionSpec as P

KRYLOV = 3
MESH = pl.DeviceIdType.MESH
LANES = 128
ROWS = 16

epsilon = 1e-12

WIRE = ("A1", "A3", "Z0", "A2", "B1", "B3", "Z1", "Z3", "C2")
PLACES = [(dz, dy) for dz in range(2) for dy in range(4)]


def least_squares(upper, initial, zero):
    target = [initial] + [zero for row_index in range(KRYLOV)]
    cosines = []
    sines = []
    for col_index in range(KRYLOV):
        for row_index in range(col_index):
            first = upper[row_index][col_index]
            second = upper[row_index + 1][col_index]
            upper[row_index][col_index] = cosines[row_index] * first + sines[row_index] * second
            upper[row_index + 1][col_index] = cosines[row_index] * second - sines[row_index] * first
        first = upper[col_index][col_index]
        second = upper[col_index + 1][col_index]
        radius = jnp.sqrt(first * first + second * second)
        cosine = first / radius
        sine_value = second / radius
        upper[col_index][col_index] = radius
        target[col_index + 1] = -sine_value * target[col_index]
        target[col_index] = cosine * target[col_index]
        cosines.append(cosine)
        sines.append(sine_value)
    combo = [None] * KRYLOV
    for row_index in reversed(range(KRYLOV)):
        running = target[row_index]
        for col_index in range(row_index + 1, KRYLOV):
            running = running - upper[row_index][col_index] * combo[col_index]
        combo[row_index] = running / upper[row_index][row_index]
    return combo


def gram_schmidt(gram, shift, initial):
    size = KRYLOV + 1

    def inner(first, second):
        total = None
        for i in range(size):
            if first[i] is None:
                continue
            row = None
            for k in range(size):
                if second[k] is None:
                    continue
                term = gram[min(i, k)][max(i, k)] * second[k]
                row = term if row is None else row + term
            term = first[i] * row
            total = term if total is None else total + term
        return total

    one = jnp.ones_like(initial)
    zero = jnp.zeros_like(initial)
    basis = [[one, None, None, None]]
    hessenberg = [[zero for col in range(KRYLOV)] for row in range(size)]
    for section in range(KRYLOV):
        current = basis[section]
        mapped = [None] * size
        for i in range(size):
            if current[i] is not None:
                own = shift * current[i]
                mapped[i] = own if mapped[i] is None else mapped[i] + own
                mapped[i + 1] = current[i]
        coefficients = [inner(basis[i], mapped) for i in range(section + 1)]
        for i in range(section + 1):
            hessenberg[i][section] = coefficients[i]
            for k in range(size):
                if basis[i][k] is not None:
                    mapped[k] = mapped[k] - coefficients[i] * basis[i][k]
        length = jnp.sqrt(jnp.maximum(inner(mapped, mapped), 0.0) + epsilon)
        hessenberg[section + 1][section] = length
        basis.append([None if value is None else value / length for value in mapped])
    combo = least_squares([list(row) for row in hessenberg], initial, zero)
    weights = []
    for k in range(KRYLOV):
        total = None
        for section in range(KRYLOV):
            if basis[section][k] is not None:
                term = combo[section] * basis[section][k]
                total = term if total is None else total + term
        weights.append(total)
    return hessenberg, weights


def kernel(
    col_ref,
    wall_ref,
    right_ref,
    relax_ref,
    drift_ref,
    sign_ref,
    blocks_ref,
    out_ref,
    hess_ref,
    weights,
    base,
    tile_one,
    tile_two,
    gather_one,
    gather_two,
    face_out,
    face_in,
    open_ref,
    w_sem,
    bulk_send,
    bulk_recv,
    pass_send,
    pass_recv,
    face_send,
    face_recv,
    one_send,
    one_recv,
    two_send,
    two_recv,
    *slots,
):
    krylov = slots[: KRYLOV + 1]
    held = [
        {(dz, dy, dc): slots[KRYLOV + 1 + 16 * j + 8 * dc + 4 * dz + dy] for dz, dy in PLACES for dc in range(2)}
        for j in range(KRYLOV)
    ]
    local_blocks = col_ref.shape[0]
    halves = (local_blocks - local_blocks // 2, local_blocks // 2)
    starts = (0, halves[0])

    mode = lax.axis_index("mode")
    gx = lax.axis_index("gx")
    gy = lax.axis_index("gy")
    zh = mode // 8
    y = (mode // 2) % 4
    core = mode % 2

    def mode_of(dz, dy, dc):
        return lax.rem(zh + dz, 2) * 8 + lax.rem(y + dy, 4) * 2 + lax.rem(core + dc, 2)

    def lanes_of(b):
        return pl.ds(pl.multiple_of(b * LANES, LANES), LANES)

    def weight_copies(dz, dy, dc):
        owner = mode_of(dz, dy, dc)
        place = 8 * dc + 4 * dz + dy
        return [
            pltpu.make_async_copy(
                blocks_ref.at[:, owner * 2 + s],
                weights.at[place, :, :, pl.ds(s * LANES, LANES)],
                w_sem.at[place, s],
            )
            for s in range(2)
        ]

    order = [
        (0, 0, 0), (0, 0, 1), (0, 1, 0), (0, 3, 0), (1, 0, 0), (0, 1, 1), (0, 3, 1), (1, 0, 1),
        (0, 2, 0), (0, 2, 1), (1, 1, 0), (1, 3, 0), (1, 1, 1), (1, 3, 1), (1, 2, 0), (1, 2, 1),
    ]
    for place in order:
        for copy in weight_copies(*place):
            copy.start()

    barrier = pltpu.get_barrier_semaphore()
    for d in range(1, 16):
        pl.semaphore_signal(barrier, inc=1, device_id={"mode": lax.rem(mode + d, 16)}, device_id_type=MESH)
    for d in range(1, 8):
        pl.semaphore_signal(
            barrier, inc=1, device_id={"gx": lax.rem(gx + d // 4, 2), "gy": lax.rem(gy + d % 4, 4)}, device_id_type=MESH
        )

    def norm_block(b, carry):
        plain, weighted = carry
        lanes = lanes_of(b)
        diagonal = relax_ref[0:1, lanes] + drift_ref[0:1, lanes] + drift_ref[1:2, lanes]
        for x in range(8):
            value = right_ref[x, :, lanes]
            square = value * value
            plain = plain + square
            weighted = weighted + square * diagonal
        return plain, weighted

    empty = jnp.zeros((8, LANES), jnp.float32)
    plain, weighted = lax.fori_loop(0, local_blocks, norm_block, (empty, empty))
    for x in range(8):
        for cell in range(8):
            open_ref[pl.ds(x * 8 + cell, 1), :] = jnp.full(
                (1, LANES), (1 - wall_ref[x, cell]).astype(jnp.float32), jnp.float32
            )

    pl.semaphore_wait(barrier, 22)

    def summed(which, rows):
        tile = jnp.concatenate(
            [jnp.sum(row, axis=0, keepdims=True) for row in rows]
            + [jnp.zeros((ROWS - len(rows), LANES), jnp.float32)],
            axis=0,
        )
        tile_one[which] = tile
        gather_one[which, mode] = tile
        copies = []
        for d in range(1, 16):
            copies.append(
                pltpu.make_async_remote_copy(
                    src_ref=tile_one.at[which],
                    dst_ref=gather_one.at[which, mode],
                    send_sem=one_send.at[which, d],
                    recv_sem=one_recv.at[which, d],
                    device_id={"mode": lax.rem(mode + d, 16)},
                    device_id_type=MESH,
                )
            )
        for copy in copies:
            copy.start()
        for copy in copies:
            copy.wait()
        total = gather_one[which, 0]
        for source in range(1, 16):
            total = total + gather_one[which, source]
        group = gx * 4 + gy
        tile_two[which] = total
        gather_two[which, group] = total
        copies = []
        for d in range(1, 8):
            copies.append(
                pltpu.make_async_remote_copy(
                    src_ref=tile_two.at[which],
                    dst_ref=gather_two.at[which, group],
                    send_sem=two_send.at[which, d],
                    recv_sem=two_recv.at[which, d],
                    device_id={"gx": lax.rem(gx + d // 4, 2), "gy": lax.rem(gy + d % 4, 4)},
                    device_id_type=MESH,
                )
            )
        for copy in copies:
            copy.start()
        for copy in copies:
            copy.wait()
        total = gather_two[which, 0]
        for source in range(1, 8):
            total = total + gather_two[which, source]
        total = jnp.broadcast_to(jnp.sum(total, axis=1, keepdims=True), (ROWS, LANES))
        tile_one[which] = total
        return [tile_one[which, pl.ds(k, 1), :] for k in range(len(rows))]

    squared, diagonal = summed(0, [plain, weighted])
    initial = jnp.sqrt(squared + epsilon)
    shift = diagonal / (squared + epsilon)

    def first_block(b, carry):
        lanes = lanes_of(b)
        value = (right_ref[:, :, lanes] / initial).reshape(64, LANES)
        krylov[0][b] = value
        held[0][0, 0, 0][b] = value.astype(jnp.bfloat16)
        return carry

    lax.fori_loop(0, local_blocks, first_block, 0)

    sends = []
    rows8 = lax.broadcasted_iota(jnp.int32, (8, LANES), 0)
    grams = {}

    for j in range(KRYLOV):
        x = held[j]
        now = krylov[j]
        later = krylov[j + 1]

        def wire(name, half, source, target, to):
            part = pl.ds(starts[half], halves[half])
            index = WIRE.index(name)
            return pltpu.make_async_remote_copy(
                src_ref=x[source].at[part],
                dst_ref=x[target].at[part],
                send_sem=bulk_send.at[j, index, half],
                recv_sem=bulk_recv.at[j, index, half],
                device_id={"mode": to},
                device_id_type=MESH,
            )

        below, above, across, beside = mode_of(0, 3, 0), mode_of(0, 1, 0), mode_of(1, 0, 0), mode_of(0, 0, 1)
        routes = {
            "A1": ((0, 0, 0), (0, 1, 0), below),
            "A3": ((0, 0, 0), (0, 3, 0), above),
            "Z0": ((0, 0, 0), (1, 0, 0), across),
            "B1": ((1, 0, 0), (1, 1, 0), below),
            "B3": ((1, 0, 0), (1, 3, 0), above),
            "Z1": ((0, 1, 0), (1, 1, 0), across),
            "Z3": ((0, 3, 0), (1, 3, 0), across),
        }

        def copy_of(name, half):
            if name == "A2":
                source, target, to = ((0, 1, 0), (0, 2, 0), below) if half == 0 else ((0, 3, 0), (0, 2, 0), above)
            elif name == "C2":
                source, target, to = ((1, 3, 0), (1, 2, 0), above) if half == 0 else ((1, 1, 0), (1, 2, 0), below)
            else:
                source, target, to = routes[name]
            return wire(name, half, source, target, to)

        def passing(dz, dy, half):
            part = pl.ds(starts[half], halves[half])
            return pltpu.make_async_remote_copy(
                src_ref=x[dz, dy, 0].at[part],
                dst_ref=x[dz, dy, 1].at[part],
                send_sem=pass_send.at[j, 4 * dz + dy, half],
                recv_sem=pass_recv.at[j, 4 * dz + dy, half],
                device_id={"mode": beside},
                device_id_type=MESH,
            )

        def start(copy):
            copy.start()
            sends.append(copy)

        def take(name, half, place, then=()):
            copy_of(name, half).wait_recv()
            for following in then:
                start(copy_of(following, half))
            start(passing(*place, half))

        for half in range(2):
            for name in ("A1", "A3", "Z0"):
                start(copy_of(name, half))
            start(passing(0, 0, half))

        def face_block(b, carry):
            low, high = now[b, 0:8, :] * open_ref[0:8, :], now[b, 56:64, :] * open_ref[56:64, :]
            face_out[j, 0, b] = jnp.where(gx == 0, high, low)
            for cell in range(8):
                value = now[b, 8 * cell : 8 * cell + 8, :] * open_ref[8 * cell : 8 * cell + 8, :]
                face_out[j, 1, b, pl.ds(cell, 1), :] = value[7:8, :]
                face_out[j, 2, b, pl.ds(cell, 1), :] = value[0:1, :]
            return carry

        lax.fori_loop(0, local_blocks, face_block, 0)
        faces = []
        for side, to in (
            (0, {"gx": lax.rem(gx + 1, 2)}),
            (1, {"gy": lax.rem(gy + 1, 4)}),
            (2, {"gy": lax.rem(gy + 3, 4)}),
        ):
            copy = pltpu.make_async_remote_copy(
                src_ref=face_out.at[j, side],
                dst_ref=face_in.at[j, side],
                send_sem=face_send.at[j, side],
                recv_sem=face_recv.at[j, side],
                device_id=to,
                device_id_type=MESH,
            )
            start(copy)
            faces.append(copy)

        def product(place, b):
            owner = mode_of(*place)
            first, second = (
                jnp.clip(col_ref[b, owner * 2 + s] - owner * local_blocks, 0, local_blocks - 1) for s in range(2)
            )
            ref = x[place]
            picked = jnp.concatenate([ref[first], ref[second]], axis=1)
            matrix = weights[8 * place[2] + 4 * place[0] + place[1], b]
            return lax.dot_general(picked, matrix, (((1,), (1,)), ((), ())), preferred_element_type=jnp.float32)

        def ready(place):
            if j == 0:
                for copy in weight_copies(*place):
                    copy.wait()
            if place[2] == 1:
                for half in range(2):
                    passing(place[0], place[1], half).wait_recv()

        def compute(place):
            ready(place)

            def block(b, carry):
                later[b] = later[b] - product(place, b)
                return carry

            lax.fori_loop(0, local_blocks, block, 0)

        def compute_first(place):
            ready(place)

            def block(b, carry):
                later[b] = -product(place, b)
                return carry

            lax.fori_loop(0, local_blocks, block, 0)

        def local_terms():
            for copy in faces:
                copy.wait_recv()

            def block(b, carry):
                lanes = lanes_of(b)
                relax = relax_ref[0:1, lanes] - shift
                speed_first, speed_second = drift_ref[0:1, lanes], drift_ref[1:2, lanes]
                to_higher_first = sign_ref[0:1, lanes] == 1
                to_higher_second = sign_ref[1:2, lanes] == 1
                edge = face_in[j, 0, b]
                values = [now[b, 8 * cell : 8 * cell + 8, :] for cell in range(8)]
                masked = [values[cell] * open_ref[8 * cell : 8 * cell + 8, :] for cell in range(8)]
                west = [jnp.where(gx == 1, edge, 0.0)] + masked[:7]
                east = masked[1:] + [jnp.where(gx == 0, edge, 0.0)]
                for cell in range(8):
                    rows = slice(8 * cell, 8 * cell + 8)
                    from_low = jnp.where(gy > 0, face_in[j, 1, b, pl.ds(cell, 1), :], 0.0)
                    from_high = jnp.where(gy < 3, face_in[j, 2, b, pl.ds(cell, 1), :], 0.0)
                    south = jnp.where(rows8 == 0, from_low, pltpu.roll(masked[cell], 1, 0))
                    north = jnp.where(rows8 == 7, from_high, pltpu.roll(masked[cell], 7, 0))
                    upstream_first = jnp.where(to_higher_first, west[cell], east[cell])
                    upstream_second = jnp.where(to_higher_second, south, north)
                    value = values[cell]
                    term = speed_first * (value - upstream_first) + speed_second * (value - upstream_second)
                    later[b, rows, :] = later[b, rows, :] + (relax * value + term)
                return carry

            lax.fori_loop(0, local_blocks, block, 0)

        def dots_with(k):
            def block(b, carry):
                totals = list(carry)
                for cell in range(8):
                    rows = slice(8 * cell, 8 * cell + 8)
                    value = krylov[k][b, rows, :]
                    for i in range(k + 1):
                        totals[i] = totals[i] + krylov[i][b, rows, :] * value
                return tuple(totals)

            totals = lax.fori_loop(0, local_blocks, block, tuple(empty for i in range(k + 1)))
            for i in range(k + 1):
                grams[i, k] = totals[i]

        compute_first((0, 0, 0))
        take("A1", 0, (0, 1), ("A2", "Z1"))
        take("A3", 0, (0, 3))
        compute((0, 0, 1))
        take("Z0", 0, (1, 0), ("B3",))
        take("A1", 1, (0, 1))
        take("A3", 1, (0, 3), ("A2", "Z3"))
        compute((0, 1, 0))
        compute((0, 3, 0))
        take("Z0", 1, (1, 0), ("B1",))
        compute((1, 0, 0))
        compute((0, 1, 1))
        take("A2", 0, (0, 2))
        take("A2", 1, (0, 2))
        compute((0, 3, 1))
        take("B3", 0, (1, 3), ("C2",))
        compute((1, 0, 1))
        local_terms()
        take("B1", 1, (1, 1), ("C2",))
        compute((0, 2, 0))
        dots_with(j)
        compute((0, 2, 1))
        take("Z1", 0, (1, 1))
        take("Z3", 1, (1, 3))
        compute((1, 1, 0))
        compute((1, 3, 0))
        take("C2", 0, (1, 2))
        take("C2", 1, (1, 2))
        compute((1, 1, 1))
        compute((1, 3, 1))
        compute((1, 2, 0))
        place = (1, 2, 1)
        ready(place)
        if j < KRYLOV - 1:
            nearby = held[j + 1][0, 0, 0]

            def last_block(b, carry):
                value = later[b] - product(place, b)
                later[b] = value
                nearby[b] = value.astype(jnp.bfloat16)
                return carry

            lax.fori_loop(0, local_blocks, last_block, 0)
        else:

            def final_block(b, carry):
                totals = list(carry)
                value = later[b] - product(place, b)
                for cell in range(8):
                    rows = slice(8 * cell, 8 * cell + 8)
                    part = value[rows, :]
                    for i in range(KRYLOV):
                        totals[i] = totals[i] + krylov[i][b, rows, :] * part
                    totals[KRYLOV] = totals[KRYLOV] + part * part
                return tuple(totals)

            totals = lax.fori_loop(0, local_blocks, final_block, tuple(empty for i in range(KRYLOV + 1)))
            for i in range(KRYLOV + 1):
                grams[i, KRYLOV] = totals[i]

    pairs = [(i, k) for k in range(KRYLOV + 1) for i in range(k + 1)]
    sums = dict(zip(pairs, summed(1, [grams[pair] for pair in pairs])))
    gram = [[sums.get((i, k)) for k in range(KRYLOV + 1)] for i in range(KRYLOV + 1)]
    hessenberg, factors = gram_schmidt(gram, shift, initial)

    def out_block(b, carry):
        lanes = lanes_of(b)
        value = factors[0] * krylov[0][b]
        for k in range(1, KRYLOV):
            value = value + factors[k] * krylov[k][b]
        out_ref[:, :, lanes] = value.reshape(8, 8, LANES)
        return carry

    lax.fori_loop(0, local_blocks, out_block, 0)
    columns = lax.broadcasted_iota(jnp.int32, (8, LANES), 1)
    tile = empty
    for i in range(KRYLOV + 1):
        for k in range(KRYLOV):
            tile = jnp.where((rows8 == i) & (columns == k), hessenberg[i][k], tile)
    hess_ref[...] = tile[: KRYLOV + 1, :KRYLOV]
    for copy in sends:
        copy.wait_send()


def per_device(right_side, col_block, blocks, relax_rate, drift_speed, upwind_sign, wall_mask):
    cells_first, cells_second, local_modes = right_side.shape
    cells = cells_first * cells_second
    local_blocks = col_block.shape[0]
    block = blocks.shape[2]
    vector = pltpu.VMEM((local_blocks, cells, block), jnp.float32)
    rounded = pltpu.VMEM((local_blocks, cells, block), jnp.bfloat16)
    dma = pltpu.SemaphoreType.DMA
    vmem = pl.BlockSpec(memory_space=pltpu.VMEM)
    smem = pl.BlockSpec(memory_space=pltpu.SMEM)
    return pl.pallas_call(
        kernel,
        out_shape=(
            jax.ShapeDtypeStruct(right_side.shape, jnp.float32),
            jax.ShapeDtypeStruct((KRYLOV + 1, KRYLOV), jnp.float32),
        ),
        in_specs=[smem, smem, vmem, vmem, vmem, vmem, pl.BlockSpec(memory_space=pl.ANY)],
        out_specs=(vmem, vmem),
        scratch_shapes=[
            pltpu.VMEM((16, local_blocks, block, 2 * block), jnp.bfloat16),
            pltpu.VMEM((8, LANES), jnp.float32),
            pltpu.VMEM((2, ROWS, LANES), jnp.float32),
            pltpu.VMEM((2, ROWS, LANES), jnp.float32),
            pltpu.VMEM((2, 16, ROWS, LANES), jnp.float32),
            pltpu.VMEM((2, 8, ROWS, LANES), jnp.float32),
            pltpu.VMEM((KRYLOV, 3, local_blocks, 8, LANES), jnp.float32),
            pltpu.VMEM((KRYLOV, 3, local_blocks, 8, LANES), jnp.float32),
            pltpu.VMEM((cells, LANES), jnp.float32),
            dma((16, 2)),
            dma((KRYLOV, len(WIRE), 2)),
            dma((KRYLOV, len(WIRE), 2)),
            dma((KRYLOV, 8, 2)),
            dma((KRYLOV, 8, 2)),
            dma((KRYLOV, 3)),
            dma((KRYLOV, 3)),
            dma((2, 16)),
            dma((2, 16)),
            dma((2, 8)),
            dma((2, 8)),
        ]
        + [vector] * (KRYLOV + 1)
        + [rounded] * (16 * KRYLOV),
        compiler_params=pltpu.CompilerParams(
            collective_id=0, has_side_effects=True, vmem_limit_bytes=60000000
        ),
        name="cycle",
    )(col_block, wall_mask, right_side, relax_rate.reshape(1, -1), drift_speed, upwind_sign, blocks)


def solution(mesh):
    return jax.shard_map(
        per_device,
        mesh=mesh,
        in_specs=(
            P("gx", "gy", "mode"),
            P("mode", None),
            P("mode", None, None, None),
            P("mode"),
            P(None, "mode"),
            P(None, "mode"),
            P("gx", "gy"),
        ),
        out_specs=(P("gx", "gy", "mode"), P()),
        check_vma=False,
    )
```

time: 992 us -> 152 us (0.15); the launches traced: 979 us -> 151 us
  blocking collectives: 644 us -> 0 us
  Pallas kernels: 0 us -> 146 us
  waiting for transfers between devices: 108 us -> 0 us
  local copies, waits for them, and re-layouts: 83.4 us -> 4.37 us
  other arithmetic: 45.7 us -> 0 us
  matrix products: 37 us -> 0 us
  starting transfers between devices: 35.2 us -> 0 us
  between operations: 26 us -> 0.64 us
    psum x10 -> x0, blocking collectives: 644 us -> none  [the longest x6 385 us: per_device(): lax.psum(jnp.sum(krylov_basis[earlier] * mapped), ('mode', 'gx', 'gy'))]
    pallas_call x0 -> x1, Pallas kernels: none -> 146 us  [per_device(): pl.pallas_call(kernel, out_shape=(jax.ShapeDtypeStruct(right_side.shape,...]
    all_gather x3 -> x0, waiting for transfers between devices: 105 us -> none  [apply_operator(): gathered = lax.all_gather(rounded, 'mode', axis=1, tiled=True)]
    gather x3 -> x0, local copies, waits for them, and re-layouts: 65 us -> none  [apply_operator(): picked = jnp.take(gathered, col_block.reshape(-1), axis=1)]
    dot_general x3 -> x0, matrix products: 37 us -> none  [apply_operator(): jnp.einsum('rsik,crsk->cri', blocks, picked, preferred_element_type=jnp.f...]
    ppermute x12 -> x0, starting transfers between devices: 35 us -> none  [the longest x6 27.3 us: extended(): lax.ppermute(lax.slice_in_dim(block, block.shape[dim] - width, None, axis...]
    select_n x4 -> x0, other arithmetic: 21.1 us -> none  [apply_operator(): picked = jnp.take(gathered, col_block.reshape(-1), axis=1)]
    reshape x7 -> x1, local copies, waits for them, and re-layouts: 16 us -> 1.3 us  [per_device(): relax_rate.reshape(1, -1)]
  transfers between devices with their start and end apart: 15 -> 0, of which waited for: 7 -> 0; matrix products, arithmetic and copies ran while one was open for 15% -> 0% of each run, Pallas kernels for 0% -> 0%
where the time goes in v1:
time: 152 us; the launch traced here: 151 us
  Pallas kernels  146 us (96%)
  local copies, waits for them, and re-layouts  4.37 us (3%)
    pallas_call x1, Pallas kernels, per_device(): pl.pallas_call(kernel, out_shape=(jax.ShapeDtypeStruct(right_side.shape,...  146 us
    unnamed x2, local copies, waits for them, and re-layouts  3.07 us

profile of v1, /device:TPU:0, one launch (start us, length us, event | category | flops | bytes accessed | tf_op | source)
XLA Modules:
  0.0 151.0 jit_solution(11706680360204198760)
XLA Ops:
  0.6 1.3 reshape.7.relax_ref
  1.9 146.0 %cycle.1 = (f32[8,8,1792]{2,1,0:T(8,128)}, f32[4,3]{1,0:T(4,128)}) custom-call(s32[14,32]{1,0:T(8,128)} %col_ref.1, s32[8,8]{1,0:T(8,128)} %wall_ref.1, f32[8,8,1792]{2,1,0:T(8,128)} %right_ref.1, f32[1,1792]{1,0:T(1,128)} %reshape.7.relax_ref, f32[2,1792]{1,0:T(2,128)} %drift_ref.1, s32[2,1792]{1,0:T(2,128)} %sign_ref.1, bf16[14,32,128,128]{3,2,1,0:T(8,128)(2,1)} %blocks_ref.1), custom_call_target="tpu_custom_call" | custom-call | tf_op jit(solution)/shard_map/cycle/pallas_call | solution.py:538
  148.0 1.8 %copy.11 = f32[8,8,1792]{2,1,0:T(8,128)} copy(f32[8,8,1792]{2,1,0:T(8,128)} %get-tuple-element.4) | data formatting | bytes 917504
  149.8 1.3 copy.12

commit v2 on v1

--- a/solution.py
+++ b/solution.py
@@ -10,11 +10,11 @@
 KRYLOV = 3
 MESH = pl.DeviceIdType.MESH
 LANES = 128
-ROWS = 16
+QUARTERS = 4
 
 epsilon = 1e-12
 
-WIRE = ("A1", "A3", "Z0", "A2", "B1", "B3", "Z1", "Z3", "C2")
+WIRE = ("A1", "A3", "Z0", "A2", "B", "Z", "C2")
 PLACES = [(dz, dy) for dz in range(2) for dy in range(4)]
 
 
@@ -99,17 +99,22 @@
 
 
 def kernel(
+    col_hbm,
+    wall_hbm,
+    right_hbm,
+    relax_hbm,
+    drift_hbm,
+    sign_hbm,
+    blocks_ref,
+    out_ref,
+    hess_ref,
     col_ref,
     wall_ref,
     right_ref,
     relax_ref,
     drift_ref,
     sign_ref,
-    blocks_ref,
-    out_ref,
-    hess_ref,
     weights,
-    base,
     tile_one,
     tile_two,
     gather_one,
@@ -117,6 +122,7 @@
     face_out,
     face_in,
     open_ref,
+    in_sem,
     w_sem,
     bulk_send,
     bulk_recv,
@@ -136,8 +142,9 @@
         for j in range(KRYLOV)
     ]
     local_blocks = col_ref.shape[0]
-    halves = (local_blocks - local_blocks // 2, local_blocks // 2)
-    starts = (0, halves[0])
+    ends = [-(-local_blocks * (q + 1) // QUARTERS) for q in range(QUARTERS)]
+    starts = [0] + ends[:-1]
+    parts = [pl.ds(start, end - start) for start, end in zip(starts, ends)]
 
     mode = lax.axis_index("mode")
     gx = lax.axis_index("gx")
@@ -145,6 +152,7 @@
     zh = mode // 8
     y = (mode // 2) % 4
     core = mode % 2
+    z = zh * 2 + gx
 
     def mode_of(dz, dy, dc):
         return lax.rem(zh + dz, 2) * 8 + lax.rem(y + dy, 4) * 2 + lax.rem(core + dc, 2)
@@ -168,22 +176,42 @@
         (0, 0, 0), (0, 0, 1), (0, 1, 0), (0, 3, 0), (1, 0, 0), (0, 1, 1), (0, 3, 1), (1, 0, 1),
         (0, 2, 0), (0, 2, 1), (1, 1, 0), (1, 3, 0), (1, 1, 1), (1, 3, 1), (1, 2, 0), (1, 2, 1),
     ]
+    ring = []
+    for d in range(1, 8):
+        z_to = lax.rem(z + d // 2, 4)
+        ring.append({"mode": z_to // 2 * 8 + y * 2 + lax.rem(core + d % 2, 2), "gx": lax.rem(z_to, 2)})
+    plane = [
+        {"mode": zh * 8 + lax.rem(y + d // 4, 4) * 2 + core, "gy": lax.rem(gy + d % 4, 4)} for d in range(1, 16)
+    ]
+    barrier = pltpu.get_barrier_semaphore()
+    for partner in plane + ring:
+        pl.semaphore_signal(barrier, inc=1, device_id=partner, device_id_type=MESH)
+
+    inputs = [
+        pltpu.make_async_copy(source, target, in_sem.at[index])
+        for index, (source, target) in enumerate(
+            (
+                (right_hbm, right_ref),
+                (relax_hbm, relax_ref),
+                (drift_hbm, drift_ref),
+                (sign_hbm, sign_ref),
+                (wall_hbm, wall_ref),
+                (col_hbm, col_ref),
+            )
+        )
+    ]
+    for copy in inputs:
+        copy.start()
     for place in order:
         for copy in weight_copies(*place):
             copy.start()
-
-    barrier = pltpu.get_barrier_semaphore()
-    for d in range(1, 16):
-        pl.semaphore_signal(barrier, inc=1, device_id={"mode": lax.rem(mode + d, 16)}, device_id_type=MESH)
-    for d in range(1, 8):
-        pl.semaphore_signal(
-            barrier, inc=1, device_id={"gx": lax.rem(gx + d // 4, 2), "gy": lax.rem(gy + d % 4, 4)}, device_id_type=MESH
-        )
+    for copy in inputs:
+        copy.wait()
 
     def norm_block(b, carry):
         plain, weighted = carry
         lanes = lanes_of(b)
-        diagonal = relax_ref[0:1, lanes] + drift_ref[0:1, lanes] + drift_ref[1:2, lanes]
+        diagonal = relax_ref[lanes][None, :] + drift_ref[0:1, lanes] + drift_ref[1:2, lanes]
         for x in range(8):
             value = right_ref[x, :, lanes]
             square = value * value
@@ -201,58 +229,42 @@
 
     pl.semaphore_wait(barrier, 22)
 
-    def summed(which, rows):
-        tile = jnp.concatenate(
-            [jnp.sum(row, axis=0, keepdims=True) for row in rows]
-            + [jnp.zeros((ROWS - len(rows), LANES), jnp.float32)],
-            axis=0,
-        )
-        tile_one[which] = tile
-        gather_one[which, mode] = tile
-        copies = []
-        for d in range(1, 16):
-            copies.append(
-                pltpu.make_async_remote_copy(
-                    src_ref=tile_one.at[which],
-                    dst_ref=gather_one.at[which, mode],
-                    send_sem=one_send.at[which, d],
-                    recv_sem=one_recv.at[which, d],
-                    device_id={"mode": lax.rem(mode + d, 16)},
-                    device_id_type=MESH,
-                )
-            )
+    lane = lax.broadcasted_iota(jnp.int32, (1, LANES), 1)
+
+    def exchanged(which, value, partners, me, count, tile, slots_of, send, recv):
+        tile[which] = value
+        slots_of[which, me] = value
+        copies = [
+            pltpu.make_async_remote_copy(
+                src_ref=tile.at[which],
+                dst_ref=slots_of.at[which, me],
+                send_sem=send.at[which, index],
+                recv_sem=recv.at[which, index],
+                device_id=partner,
+                device_id_type=MESH,
+            )
+            for index, partner in enumerate(partners)
+        ]
         for copy in copies:
             copy.start()
         for copy in copies:
             copy.wait()
-        total = gather_one[which, 0]
-        for source in range(1, 16):
-            total = total + gather_one[which, source]
-        group = gx * 4 + gy
-        tile_two[which] = total
-        gather_two[which, group] = total
-        copies = []
-        for d in range(1, 8):
-            copies.append(
-                pltpu.make_async_remote_copy(
-                    src_ref=tile_two.at[which],
-                    dst_ref=gather_two.at[which, group],
-                    send_sem=two_send.at[which, d],
-                    recv_sem=two_recv.at[which, d],
-                    device_id={"gx": lax.rem(gx + d // 4, 2), "gy": lax.rem(gy + d % 4, 4)},
-                    device_id_type=MESH,
-                )
-            )
-        for copy in copies:
-            copy.start()
-        for copy in copies:
-            copy.wait()
-        total = gather_two[which, 0]
-        for source in range(1, 8):
-            total = total + gather_two[which, source]
-        total = jnp.broadcast_to(jnp.sum(total, axis=1, keepdims=True), (ROWS, LANES))
-        tile_one[which] = total
-        return [tile_one[which, pl.ds(k, 1), :] for k in range(len(rows))]
+        total = slots_of[which, 0]
+        for source in range(1, count):
+            total = total + slots_of[which, source]
+        return total
+
+    def summed(which, partials):
+        packed = jnp.zeros((1, LANES), jnp.float32)
+        for k, partial in enumerate(partials):
+            own = jnp.sum(jnp.sum(partial, axis=0, keepdims=True), axis=1, keepdims=True)
+            packed = jnp.where(lane == k, own, packed)
+        packed = exchanged(which, packed, ring, z * 2 + core, 8, tile_one, gather_one, one_send, one_recv)
+        packed = exchanged(which, packed, plane, y * 4 + gy, 16, tile_two, gather_two, two_send, two_recv)
+        return [
+            jnp.broadcast_to(jnp.sum(jnp.where(lane == k, packed, 0.0), axis=1, keepdims=True), (1, LANES))
+            for k in range(len(partials))
+        ]
 
     squared, diagonal = summed(0, [plain, weighted])
     initial = jnp.sqrt(squared + epsilon)
@@ -276,45 +288,51 @@
         now = krylov[j]
         later = krylov[j + 1]
 
-        def wire(name, half, source, target, to):
-            part = pl.ds(starts[half], halves[half])
+        below, above, across, beside = mode_of(0, 3, 0), mode_of(0, 1, 0), mode_of(1, 0, 0), mode_of(0, 0, 1)
+
+        def route(name, q):
+            first = q < 2
+            return {
+                "A1": ((0, 0), (0, 1), below),
+                "A3": ((0, 0), (0, 3), above),
+                "Z0": ((0, 0), (1, 0), across),
+                "A2": ((0, 1), (0, 2), below) if first else ((0, 3), (0, 2), above),
+                "B": ((1, 0), (1, 3), above) if first else ((1, 0), (1, 1), below),
+                "Z": ((0, 1), (1, 1), across) if first else ((0, 3), (1, 3), across),
+                "C2": ((1, 3), (1, 2), above) if first else ((1, 1), (1, 2), below),
+            }[name]
+
+        def copy_of(name, q):
+            source, target, to = route(name, q)
             index = WIRE.index(name)
             return pltpu.make_async_remote_copy(
-                src_ref=x[source].at[part],
-                dst_ref=x[target].at[part],
-                send_sem=bulk_send.at[j, index, half],
-                recv_sem=bulk_recv.at[j, index, half],
+                src_ref=x[source[0], source[1], 0].at[parts[q]],
+                dst_ref=x[target[0], target[1], 0].at[parts[q]],
+                send_sem=bulk_send.at[j, index],
+                recv_sem=bulk_recv.at[j, index, q],
                 device_id={"mode": to},
                 device_id_type=MESH,
             )
 
-        below, above, across, beside = mode_of(0, 3, 0), mode_of(0, 1, 0), mode_of(1, 0, 0), mode_of(0, 0, 1)
-        routes = {
-            "A1": ((0, 0, 0), (0, 1, 0), below),
-            "A3": ((0, 0, 0), (0, 3, 0), above),
-            "Z0": ((0, 0, 0), (1, 0, 0), across),
-            "B1": ((1, 0, 0), (1, 1, 0), below),
-            "B3": ((1, 0, 0), (1, 3, 0), above),
-            "Z1": ((0, 1, 0), (1, 1, 0), across),
-            "Z3": ((0, 3, 0), (1, 3, 0), across),
-        }
-
-        def copy_of(name, half):
-            if name == "A2":
-                source, target, to = ((0, 1, 0), (0, 2, 0), below) if half == 0 else ((0, 3, 0), (0, 2, 0), above)
-            elif name == "C2":
-                source, target, to = ((1, 3, 0), (1, 2, 0), above) if half == 0 else ((1, 1, 0), (1, 2, 0), below)
-            else:
-                source, target, to = routes[name]
-            return wire(name, half, source, target, to)
-
-        def passing(dz, dy, half):
-            part = pl.ds(starts[half], halves[half])
+        def passing(place, part=None):
+            dz, dy = place
+            source, target = x[dz, dy, 0], x[dz, dy, 1]
             return pltpu.make_async_remote_copy(
-                src_ref=x[dz, dy, 0].at[part],
-                dst_ref=x[dz, dy, 1].at[part],
-                send_sem=pass_send.at[j, 4 * dz + dy, half],
-                recv_sem=pass_recv.at[j, 4 * dz + dy, half],
+                src_ref=source if part is None else source.at[part],
+                dst_ref=target if part is None else target.at[part],
+                send_sem=pass_send.at[j, 4 * dz + dy],
+                recv_sem=pass_recv.at[j, 4 * dz + dy],
+                device_id={"mode": beside},
+                device_id_type=MESH,
+            )
+
+        def sent_all(index):
+            whole = x[0, 0, 0]
+            return pltpu.make_async_remote_copy(
+                src_ref=whole,
+                dst_ref=whole,
+                send_sem=bulk_send.at[j, index],
+                recv_sem=bulk_recv.at[j, index, 0],
                 device_id={"mode": beside},
                 device_id_type=MESH,
             )
@@ -323,16 +341,29 @@
             copy.start()
             sends.append(copy)
 
-        def take(name, half, place, then=()):
-            copy_of(name, half).wait_recv()
-            for following in then:
-                start(copy_of(following, half))
-            start(passing(*place, half))
-
-        for half in range(2):
-            for name in ("A1", "A3", "Z0"):
-                start(copy_of(name, half))
-            start(passing(0, 0, half))
+        following = {
+            ("A1", 0): ("A2", "Z"), ("A1", 1): ("A2", "Z"), ("A3", 2): ("A2", "Z"), ("A3", 3): ("A2", "Z"),
+            ("Z0", 0): ("B",), ("Z0", 1): ("B",), ("Z0", 2): ("B",), ("Z0", 3): ("B",),
+            ("B", 0): ("C2",), ("B", 1): ("C2",), ("B", 2): ("C2",), ("B", 3): ("C2",),
+        }
+
+        def take(name, *quarters):
+            for q in quarters:
+                copy_of(name, q).wait_recv()
+                for after in following.get((name, q), ()):
+                    copy_of(after, q).start()
+                passing(route(name, q)[1], parts[q]).start()
+
+        def send_own(quarters):
+            for q in quarters:
+                copy_of("A1", q).start()
+                copy_of("A3", q).start()
+                copy_of("Z0", (0, 2, 1, 3)[q]).start()
+                passing((0, 0), parts[q]).start()
+
+        send_own(range(QUARTERS))
+        sends.extend(sent_all(index) for index in range(len(WIRE)))
+        sends.extend(passing(place) for place in PLACES)
 
         def face_block(b, carry):
             low, high = now[b, 0:8, :] * open_ref[0:8, :], now[b, 56:64, :] * open_ref[56:64, :]
@@ -376,8 +407,7 @@
                 for copy in weight_copies(*place):
                     copy.wait()
             if place[2] == 1:
-                for half in range(2):
-                    passing(place[0], place[1], half).wait_recv()
+                passing(place[:2]).wait_recv()
 
         def compute(place):
             ready(place)
@@ -386,7 +416,7 @@
                 later[b] = later[b] - product(place, b)
                 return carry
 
-            lax.fori_loop(0, local_blocks, block, 0)
+            lax.fori_loop(0, local_blocks, block, 0, unroll=True)
 
         def compute_first(place):
             ready(place)
@@ -395,7 +425,7 @@
                 later[b] = -product(place, b)
                 return carry
 
-            lax.fori_loop(0, local_blocks, block, 0)
+            lax.fori_loop(0, local_blocks, block, 0, unroll=True)
 
         def local_terms():
             for copy in faces:
@@ -403,7 +433,7 @@
 
             def block(b, carry):
                 lanes = lanes_of(b)
-                relax = relax_ref[0:1, lanes] - shift
+                relax = relax_ref[lanes][None, :] - shift
                 speed_first, speed_second = drift_ref[0:1, lanes], drift_ref[1:2, lanes]
                 to_higher_first = sign_ref[0:1, lanes] == 1
                 to_higher_second = sign_ref[1:2, lanes] == 1
@@ -442,33 +472,44 @@
                 grams[i, k] = totals[i]
 
         compute_first((0, 0, 0))
-        take("A1", 0, (0, 1), ("A2", "Z1"))
-        take("A3", 0, (0, 3))
         compute((0, 0, 1))
-        take("Z0", 0, (1, 0), ("B3",))
-        take("A1", 1, (0, 1))
-        take("A3", 1, (0, 3), ("A2", "Z3"))
+        take("A1", 0)
+        take("A3", 0)
+        take("Z0", 0)
+        take("A1", 1)
+        take("A3", 1)
+        take("Z0", 2)
+        dots_with(j)
+        take("A1", 2)
+        take("A3", 2)
+        take("Z0", 1)
+        take("A1", 3)
+        take("A3", 3)
+        take("Z0", 3)
         compute((0, 1, 0))
+        take("B", 0)
+        take("A2", 0)
         compute((0, 3, 0))
-        take("Z0", 1, (1, 0), ("B1",))
         compute((1, 0, 0))
+        take("A2", 1, 2)
+        take("Z", 0)
         compute((0, 1, 1))
-        take("A2", 0, (0, 2))
-        take("A2", 1, (0, 2))
         compute((0, 3, 1))
-        take("B3", 0, (1, 3), ("C2",))
+        take("B", 1, 2)
+        take("Z", 1)
         compute((1, 0, 1))
         local_terms()
-        take("B1", 1, (1, 1), ("C2",))
+        take("A2", 3)
+        take("B", 3)
+        take("Z", 2)
         compute((0, 2, 0))
-        dots_with(j)
         compute((0, 2, 1))
-        take("Z1", 0, (1, 1))
-        take("Z3", 1, (1, 3))
+        take("C2", 0)
+        take("Z", 3)
+        take("C2", 2)
         compute((1, 1, 0))
         compute((1, 3, 0))
-        take("C2", 0, (1, 2))
-        take("C2", 1, (1, 2))
+        take("C2", 1, 3)
         compute((1, 1, 1))
         compute((1, 3, 1))
         compute((1, 2, 0))
@@ -483,7 +524,7 @@
                 nearby[b] = value.astype(jnp.bfloat16)
                 return carry
 
-            lax.fori_loop(0, local_blocks, last_block, 0)
+            lax.fori_loop(0, local_blocks, last_block, 0, unroll=True)
         else:
 
             def final_block(b, carry):
@@ -497,7 +538,7 @@
                     totals[KRYLOV] = totals[KRYLOV] + part * part
                 return tuple(totals)
 
-            totals = lax.fori_loop(0, local_blocks, final_block, tuple(empty for i in range(KRYLOV + 1)))
+            totals = lax.fori_loop(0, local_blocks, final_block, tuple(empty for i in range(KRYLOV + 1)), unroll=True)
             for i in range(KRYLOV + 1):
                 grams[i, KRYLOV] = totals[i]
 
@@ -534,36 +575,41 @@
     rounded = pltpu.VMEM((local_blocks, cells, block), jnp.bfloat16)
     dma = pltpu.SemaphoreType.DMA
     vmem = pl.BlockSpec(memory_space=pltpu.VMEM)
-    smem = pl.BlockSpec(memory_space=pltpu.SMEM)
     return pl.pallas_call(
         kernel,
         out_shape=(
             jax.ShapeDtypeStruct(right_side.shape, jnp.float32),
             jax.ShapeDtypeStruct((KRYLOV + 1, KRYLOV), jnp.float32),
         ),
-        in_specs=[smem, smem, vmem, vmem, vmem, vmem, pl.BlockSpec(memory_space=pl.ANY)],
+        in_specs=[pl.BlockSpec(memory_space=pl.ANY)] * 7,
         out_specs=(vmem, vmem),
         scratch_shapes=[
+            pltpu.SMEM(col_block.shape, jnp.int32),
+            pltpu.SMEM(wall_mask.shape, jnp.int32),
+            pltpu.VMEM(right_side.shape, jnp.float32),
+            pltpu.VMEM(relax_rate.shape, jnp.float32),
+            pltpu.VMEM(drift_speed.shape, jnp.float32),
+            pltpu.VMEM(upwind_sign.shape, jnp.int32),
             pltpu.VMEM((16, local_blocks, block, 2 * block), jnp.bfloat16),
-            pltpu.VMEM((8, LANES), jnp.float32),
-            pltpu.VMEM((2, ROWS, LANES), jnp.float32),
-            pltpu.VMEM((2, ROWS, LANES), jnp.float32),
-            pltpu.VMEM((2, 16, ROWS, LANES), jnp.float32),
-            pltpu.VMEM((2, 8, ROWS, LANES), jnp.float32),
+            pltpu.VMEM((2, 1, LANES), jnp.float32),
+            pltpu.VMEM((2, 1, LANES), jnp.float32),
+            pltpu.VMEM((2, 8, 1, LANES), jnp.float32),
+            pltpu.VMEM((2, 16, 1, LANES), jnp.float32),
             pltpu.VMEM((KRYLOV, 3, local_blocks, 8, LANES), jnp.float32),
             pltpu.VMEM((KRYLOV, 3, local_blocks, 8, LANES), jnp.float32),
             pltpu.VMEM((cells, LANES), jnp.float32),
+            dma((6,)),
             dma((16, 2)),
-            dma((KRYLOV, len(WIRE), 2)),
-            dma((KRYLOV, len(WIRE), 2)),
-            dma((KRYLOV, 8, 2)),
-            dma((KRYLOV, 8, 2)),
+            dma((KRYLOV, len(WIRE))),
+            dma((KRYLOV, len(WIRE), QUARTERS)),
+            dma((KRYLOV, len(PLACES))),
+            dma((KRYLOV, len(PLACES))),
             dma((KRYLOV, 3)),
             dma((KRYLOV, 3)),
-            dma((2, 16)),
-            dma((2, 16)),
-            dma((2, 8)),
-            dma((2, 8)),
+            dma((2, 7)),
+            dma((2, 7)),
+            dma((2, 15)),
+            dma((2, 15)),
         ]
         + [vector] * (KRYLOV + 1)
         + [rounded] * (16 * KRYLOV),
@@ -571,7 +617,7 @@
             collective_id=0, has_side_effects=True, vmem_limit_bytes=60000000
         ),
         name="cycle",
-    )(col_block, wall_mask, right_side, relax_rate.reshape(1, -1), drift_speed, upwind_sign, blocks)
+    )(col_block, wall_mask, right_side, relax_rate, drift_speed, upwind_sign, blocks)
 
 
 def solution(mesh):

time: 152 us -> 87.2 us (0.57)
  Pallas kernels: 146 us -> 83.3 us
    pallas_call x1, Pallas kernels: 146 us -> 83.3 us  [per_device(): pl.pallas_call(kernel, out_shape=(jax.ShapeDtypeStruct(right_side.shape,...]
where the time goes in v2:
time: 87.2 us; the launch traced here: 87 us
  Pallas kernels  83.3 us (96%)
  local copies, waits for them, and re-layouts  3.07 us (4%)
    pallas_call x1, Pallas kernels, per_device(): pl.pallas_call(kernel, out_shape=(jax.ShapeDtypeStruct(right_side.shape,...  83.3 us
    unnamed x2, local copies, waits for them, and re-layouts  3.07 us

profile of v2, /device:TPU:0, one launch (start us, length us, event | category | flops | bytes accessed | tf_op | source)
XLA Modules:
  0.0 87.0 jit_solution(15092459006613645138)
XLA Ops:
  0.6 83.3 %cycle.1 = (f32[8,8,1792]{2,1,0:T(8,128)}, f32[4,3]{1,0:T(4,128)}) custom-call(s32[14,32]{1,0:T(8,128)} %col_hbm.1, s32[8,8]{1,0:T(8,128)} %wall_hbm.1, f32[8,8,1792]{2,1,0:T(8,128)} %right_hbm.1, f32[1792]{0:T(1024)} %relax_hbm.1, f32[2,1792]{1,0:T(2,128)} %drift_hbm.1, s32[2,1792]{1,0:T(2,128)} %sign_hbm.1, bf16[14,32,128,128]{3,2,1,0:T(8,128)(2,1)} %blocks_ref.1), custom_call_target="tpu_custom_call" | custom-call | tf_op jit(solution)/shard_map/cycle/pallas_call | solution.py:578
  83.9 1.8 %copy.11 = f32[8,8,1792]{2,1,0:T(8,128)} copy(f32[8,8,1792]{2,1,0:T(8,128)} %get-tuple-element.4) | data formatting | bytes 917504
  85.7 1.3 %copy.12 = f32[4,3]{1,0:T(4,128)} copy(f32[4,3]{1,0:T(4,128)} %get-tuple-element.5) | data formatting | bytes 96

commit v3 on v2

--- a/solution.py
+++ b/solution.py
@@ -65,9 +65,8 @@
             total = term if total is None else total + term
         return total
 
-    one = jnp.ones_like(initial)
     zero = jnp.zeros_like(initial)
-    basis = [[one, None, None, None]]
+    basis = [[1.0 / initial, None, None, None]]
     hessenberg = [[zero for col in range(KRYLOV)] for row in range(size)]
     for section in range(KRYLOV):
         current = basis[section]
@@ -217,6 +216,9 @@
             square = value * value
             plain = plain + square
             weighted = weighted + square * diagonal
+        value = right_ref[:, :, lanes].reshape(64, LANES)
+        krylov[0][b] = value
+        held[0][0, 0, 0][b] = value.astype(jnp.bfloat16)
         return plain, weighted
 
     empty = jnp.zeros((8, LANES), jnp.float32)
@@ -231,13 +233,17 @@
 
     lane = lax.broadcasted_iota(jnp.int32, (1, LANES), 1)
 
-    def exchanged(which, value, partners, me, count, tile, slots_of, send, recv):
-        tile[which] = value
-        slots_of[which, me] = value
-        copies = [
+    stages = (
+        (ring, z * 2 + core, 8, tile_one, gather_one, one_send, one_recv),
+        (plane, y * 4 + gy, 16, tile_two, gather_two, two_send, two_recv),
+    )
+
+    def copies_of(which, stage):
+        partners, me, _, tile, places, send, recv = stages[stage]
+        return [
             pltpu.make_async_remote_copy(
                 src_ref=tile.at[which],
-                dst_ref=slots_of.at[which, me],
+                dst_ref=places.at[which, me],
                 send_sem=send.at[which, index],
                 recv_sem=recv.at[which, index],
                 device_id=partner,
@@ -245,61 +251,59 @@
             )
             for index, partner in enumerate(partners)
         ]
-        for copy in copies:
+
+    def post(which, stage, value):
+        _, me, _, tile, places, _, _ = stages[stage]
+        tile[which] = value
+        places[which, me] = value
+        for copy in copies_of(which, stage):
             copy.start()
-        for copy in copies:
+
+    def collect(which, stage):
+        _, _, count, _, places, _, _ = stages[stage]
+        for copy in copies_of(which, stage):
             copy.wait()
-        total = slots_of[which, 0]
+        total = places[which, 0]
         for source in range(1, count):
-            total = total + slots_of[which, source]
+            total = total + places[which, source]
         return total
 
-    def summed(which, partials):
+    def pack(partials):
         packed = jnp.zeros((1, LANES), jnp.float32)
         for k, partial in enumerate(partials):
             own = jnp.sum(jnp.sum(partial, axis=0, keepdims=True), axis=1, keepdims=True)
             packed = jnp.where(lane == k, own, packed)
-        packed = exchanged(which, packed, ring, z * 2 + core, 8, tile_one, gather_one, one_send, one_recv)
-        packed = exchanged(which, packed, plane, y * 4 + gy, 16, tile_two, gather_two, two_send, two_recv)
+        return packed
+
+    def unpack(packed, count):
         return [
             jnp.broadcast_to(jnp.sum(jnp.where(lane == k, packed, 0.0), axis=1, keepdims=True), (1, LANES))
-            for k in range(len(partials))
+            for k in range(count)
         ]
 
-    squared, diagonal = summed(0, [plain, weighted])
-    initial = jnp.sqrt(squared + epsilon)
-    shift = diagonal / (squared + epsilon)
-
-    def first_block(b, carry):
-        lanes = lanes_of(b)
-        value = (right_ref[:, :, lanes] / initial).reshape(64, LANES)
-        krylov[0][b] = value
-        held[0][0, 0, 0][b] = value.astype(jnp.bfloat16)
-        return carry
-
-    lax.fori_loop(0, local_blocks, first_block, 0)
-
+    post(0, 0, pack([plain, weighted]))
     sends = []
     rows8 = lax.broadcasted_iota(jnp.int32, (8, LANES), 0)
     grams = {}
 
-    for j in range(KRYLOV):
+    def start(copy):
+        copy.start()
+        sends.append(copy)
+
+    def gather_of(j):
         x = held[j]
-        now = krylov[j]
-        later = krylov[j + 1]
-
         below, above, across, beside = mode_of(0, 3, 0), mode_of(0, 1, 0), mode_of(1, 0, 0), mode_of(0, 0, 1)
 
         def route(name, q):
-            first = q < 2
+            even = q % 2 == 0
             return {
                 "A1": ((0, 0), (0, 1), below),
                 "A3": ((0, 0), (0, 3), above),
                 "Z0": ((0, 0), (1, 0), across),
-                "A2": ((0, 1), (0, 2), below) if first else ((0, 3), (0, 2), above),
-                "B": ((1, 0), (1, 3), above) if first else ((1, 0), (1, 1), below),
-                "Z": ((0, 1), (1, 1), across) if first else ((0, 3), (1, 3), across),
-                "C2": ((1, 3), (1, 2), above) if first else ((1, 1), (1, 2), below),
+                "A2": ((0, 1), (0, 2), below) if even else ((0, 3), (0, 2), above),
+                "B": ((1, 0), (1, 3), above) if even else ((1, 0), (1, 1), below),
+                "Z": ((0, 1), (1, 1), across) if even else ((0, 3), (1, 3), across),
+                "C2": ((1, 3), (1, 2), above) if even else ((1, 1), (1, 2), below),
             }[name]
 
         def copy_of(name, q):
@@ -337,15 +341,10 @@
                 device_id_type=MESH,
             )
 
-        def start(copy):
-            copy.start()
-            sends.append(copy)
-
-        following = {
-            ("A1", 0): ("A2", "Z"), ("A1", 1): ("A2", "Z"), ("A3", 2): ("A2", "Z"), ("A3", 3): ("A2", "Z"),
-            ("Z0", 0): ("B",), ("Z0", 1): ("B",), ("Z0", 2): ("B",), ("Z0", 3): ("B",),
-            ("B", 0): ("C2",), ("B", 1): ("C2",), ("B", 2): ("C2",), ("B", 3): ("C2",),
-        }
+        following = {("A1", 0): ("A2", "Z"), ("A1", 2): ("A2", "Z"), ("A3", 1): ("A2", "Z"), ("A3", 3): ("A2", "Z")}
+        for q in range(QUARTERS):
+            following["Z0", q] = ("B",)
+            following["B", q] = ("C2",)
 
         def take(name, *quarters):
             for q in quarters:
@@ -354,16 +353,26 @@
                     copy_of(after, q).start()
                 passing(route(name, q)[1], parts[q]).start()
 
-        def send_own(quarters):
-            for q in quarters:
-                copy_of("A1", q).start()
-                copy_of("A3", q).start()
-                copy_of("Z0", (0, 2, 1, 3)[q]).start()
-                passing((0, 0), parts[q]).start()
-
-        send_own(range(QUARTERS))
+        def send_own(q):
+            copy_of("A1", q).start()
+            copy_of("A3", q).start()
+            copy_of("Z0", q).start()
+            passing((0, 0), parts[q]).start()
+
         sends.extend(sent_all(index) for index in range(len(WIRE)))
         sends.extend(passing(place) for place in PLACES)
+        return passing, take, send_own
+
+    gathers = [gather_of(j) for j in range(KRYLOV)]
+    for q in range(QUARTERS):
+        gathers[0][2](q)
+
+    for j in range(KRYLOV):
+        x = held[j]
+        now = krylov[j]
+        later = krylov[j + 1]
+
+        passing, take, _ = gathers[j]
 
         def face_block(b, carry):
             low, high = now[b, 0:8, :] * open_ref[0:8, :], now[b, 56:64, :] * open_ref[56:64, :]
@@ -375,13 +384,8 @@
             return carry
 
         lax.fori_loop(0, local_blocks, face_block, 0)
-        faces = []
-        for side, to in (
-            (0, {"gx": lax.rem(gx + 1, 2)}),
-            (1, {"gy": lax.rem(gy + 1, 4)}),
-            (2, {"gy": lax.rem(gy + 3, 4)}),
-        ):
-            copy = pltpu.make_async_remote_copy(
+        faces = [
+            pltpu.make_async_remote_copy(
                 src_ref=face_out.at[j, side],
                 dst_ref=face_in.at[j, side],
                 send_sem=face_send.at[j, side],
@@ -389,8 +393,14 @@
                 device_id=to,
                 device_id_type=MESH,
             )
-            start(copy)
-            faces.append(copy)
+            for side, to in (
+                (0, {"gx": lax.rem(gx + 1, 2)}),
+                (1, {"gy": lax.rem(gy + 1, 4)}),
+                (2, {"gy": lax.rem(gy + 3, 4)}),
+            )
+        ]
+        start(faces[1])
+        start(faces[2])
 
         def product(place, b):
             owner = mode_of(*place)
@@ -428,7 +438,7 @@
             lax.fori_loop(0, local_blocks, block, 0, unroll=True)
 
         def local_terms():
-            for copy in faces:
+            for copy in faces[1:]:
                 copy.wait_recv()
 
             def block(b, carry):
@@ -437,11 +447,10 @@
                 speed_first, speed_second = drift_ref[0:1, lanes], drift_ref[1:2, lanes]
                 to_higher_first = sign_ref[0:1, lanes] == 1
                 to_higher_second = sign_ref[1:2, lanes] == 1
-                edge = face_in[j, 0, b]
                 values = [now[b, 8 * cell : 8 * cell + 8, :] for cell in range(8)]
                 masked = [values[cell] * open_ref[8 * cell : 8 * cell + 8, :] for cell in range(8)]
-                west = [jnp.where(gx == 1, edge, 0.0)] + masked[:7]
-                east = masked[1:] + [jnp.where(gx == 0, edge, 0.0)]
+                west = [empty] + masked[:7]
+                east = masked[1:] + [empty]
                 for cell in range(8):
                     rows = slice(8 * cell, 8 * cell + 8)
                     from_low = jnp.where(gy > 0, face_in[j, 1, b, pl.ds(cell, 1), :], 0.0)
@@ -457,6 +466,20 @@
 
             lax.fori_loop(0, local_blocks, block, 0)
 
+        def edge_terms():
+            faces[0].wait_recv()
+            rows = pl.ds(pl.multiple_of((1 - gx) * 56, 8), 8)
+
+            def block(b, carry):
+                lanes = lanes_of(b)
+                inward = sign_ref[0:1, lanes] == gx
+                later[b, rows, :] = later[b, rows, :] - jnp.where(
+                    inward, drift_ref[0:1, lanes] * face_in[j, 0, b], 0.0
+                )
+                return carry
+
+            lax.fori_loop(0, local_blocks, block, 0)
+
         def dots_with(k):
             def block(b, carry):
                 totals = list(carry)
@@ -476,55 +499,63 @@
         take("A1", 0)
         take("A3", 0)
         take("Z0", 0)
+        take("A3", 1)
         take("A1", 1)
-        take("A3", 1)
-        take("Z0", 2)
+        take("Z0", 1)
         dots_with(j)
+        if j == 0:
+            post(0, 1, collect(0, 0))
         take("A1", 2)
         take("A3", 2)
-        take("Z0", 1)
+        take("Z0", 2)
+        take("A3", 3)
         take("A1", 3)
-        take("A3", 3)
         take("Z0", 3)
+        start(faces[0])
         compute((0, 1, 0))
         take("B", 0)
         take("A2", 0)
         compute((0, 3, 0))
+        take("B", 1)
+        take("A2", 1)
         compute((1, 0, 0))
-        take("A2", 1, 2)
         take("Z", 0)
         compute((0, 1, 1))
+        take("B", 2)
+        take("A2", 2)
         compute((0, 3, 1))
-        take("B", 1, 2)
         take("Z", 1)
         compute((1, 0, 1))
+        if j == 0:
+            squared, diagonal = unpack(collect(0, 1), 2)
+            shift = diagonal / (squared + epsilon)
         local_terms()
+        take("B", 3)
         take("A2", 3)
-        take("B", 3)
         take("Z", 2)
         compute((0, 2, 0))
         compute((0, 2, 1))
-        take("C2", 0)
+        take("C2", 0, 1)
         take("Z", 3)
-        take("C2", 2)
         compute((1, 1, 0))
         compute((1, 3, 0))
-        take("C2", 1, 3)
+        take("C2", 2)
         compute((1, 1, 1))
+        take("C2", 3)
         compute((1, 3, 1))
+        edge_terms()
         compute((1, 2, 0))
         place = (1, 2, 1)
         ready(place)
         if j < KRYLOV - 1:
             nearby = held[j + 1][0, 0, 0]
 
-            def last_block(b, carry):
-                value = later[b] - product(place, b)
-                later[b] = value
-                nearby[b] = value.astype(jnp.bfloat16)
-                return carry
-
-            lax.fori_loop(0, local_blocks, last_block, 0, unroll=True)
+            for q in range(QUARTERS):
+                for b in range(starts[q], ends[q]):
+                    value = later[b] - product(place, b)
+                    later[b] = value
+                    nearby[b] = value.astype(jnp.bfloat16)
+                gathers[j + 1][2](q)
         else:
 
             def final_block(b, carry):
@@ -543,8 +574,11 @@
                 grams[i, KRYLOV] = totals[i]
 
     pairs = [(i, k) for k in range(KRYLOV + 1) for i in range(k + 1)]
-    sums = dict(zip(pairs, summed(1, [grams[pair] for pair in pairs])))
+    post(1, 0, pack([grams[pair] for pair in pairs]))
+    post(1, 1, collect(1, 0))
+    sums = dict(zip(pairs, unpack(collect(1, 1), len(pairs))))
     gram = [[sums.get((i, k)) for k in range(KRYLOV + 1)] for i in range(KRYLOV + 1)]
+    initial = jnp.sqrt(gram[0][0] + epsilon)
     hessenberg, factors = gram_schmidt(gram, shift, initial)
 
     def out_block(b, carry):

time: 87.2 us -> 77.9 us (0.89)
  Pallas kernels: 83.3 us -> 74 us
    pallas_call x1, Pallas kernels: 83.3 us -> 74 us  [per_device(): pl.pallas_call(kernel, out_shape=(jax.ShapeDtypeStruct(right_side.shape,...]
where the time goes in v3:
time: 77.9 us; the launch traced here: 77.7 us
  Pallas kernels  74 us (95%)
  local copies, waits for them, and re-layouts  3.07 us (4%)
    pallas_call x1, Pallas kernels, per_device(): pl.pallas_call(kernel, out_shape=(jax.ShapeDtypeStruct(right_side.shape,...  74 us
    unnamed x2, local copies, waits for them, and re-layouts  3.07 us

profile of v3, /device:TPU:0, one launch (start us, length us, event | category | flops | bytes accessed | tf_op | source)
XLA Modules:
  0.0 77.7 jit_solution(6405013777023724529)
XLA Ops:
  0.6 74.0 %cycle.1 = (f32[8,8,1792]{2,1,0:T(8,128)}, f32[4,3]{1,0:T(4,128)}) custom-call(s32[14,32]{1,0:T(8,128)} %col_hbm.1, s32[8,8]{1,0:T(8,128)} %wall_hbm.1, f32[8,8,1792]{2,1,0:T(8,128)} %right_hbm.1, f32[1792]{0:T(1024)} %relax_hbm.1, f32[2,1792]{1,0:T(2,128)} %drift_hbm.1, s32[2,1792]{1,0:T(2,128)} %sign_hbm.1, bf16[14,32,128,128]{3,2,1,0:T(8,128)(2,1)} %blocks_ref.1), custom_call_target="tpu_custom_call" | custom-call | tf_op jit(solution)/shard_map/cycle/pallas_call | solution.py:612
  74.7 1.8 %copy.11 = f32[8,8,1792]{2,1,0:T(8,128)} copy(f32[8,8,1792]{2,1,0:T(8,128)} %get-tuple-element.4) | data formatting | bytes 917504
  76.5 1.3 %copy.12 = f32[4,3]{1,0:T(4,128)} copy(f32[4,3]{1,0:T(4,128)} %get-tuple-element.5) | data formatting | bytes 96

commit v4 on v3

--- a/solution.py
+++ b/solution.py
@@ -515,33 +515,33 @@
         compute((0, 1, 0))
         take("B", 0)
         take("A2", 0)
+        take("A2", 1)
         compute((0, 3, 0))
         take("B", 1)
-        take("A2", 1)
         compute((1, 0, 0))
         take("Z", 0)
         compute((0, 1, 1))
         take("B", 2)
+        compute((0, 3, 1))
+        take("B", 3)
+        take("Z", 1)
         take("A2", 2)
-        compute((0, 3, 1))
-        take("Z", 1)
         compute((1, 0, 1))
+        take("A2", 3)
         if j == 0:
             squared, diagonal = unpack(collect(0, 1), 2)
             shift = diagonal / (squared + epsilon)
         local_terms()
-        take("B", 3)
-        take("A2", 3)
         take("Z", 2)
         compute((0, 2, 0))
+        take("C2", 0, 1)
         compute((0, 2, 1))
-        take("C2", 0, 1)
         take("Z", 3)
         compute((1, 1, 0))
+        take("C2", 2)
         compute((1, 3, 0))
-        take("C2", 2)
+        take("C2", 3)
         compute((1, 1, 1))
-        take("C2", 3)
         compute((1, 3, 1))
         edge_terms()
         compute((1, 2, 0))
@@ -600,6 +600,11 @@
         copy.wait_send()
 
 
+def handed_on(solution_in, hessenberg_in, solution_out, hessenberg_out):
+    solution_out[...] = solution_in[...]
+    hessenberg_out[...] = hessenberg_in[...]
+
+
 def per_device(right_side, col_block, blocks, relax_rate, drift_speed, upwind_sign, wall_mask):
     cells_first, cells_second, local_modes = right_side.shape
     cells = cells_first * cells_second
@@ -609,7 +614,7 @@
     rounded = pltpu.VMEM((local_blocks, cells, block), jnp.bfloat16)
     dma = pltpu.SemaphoreType.DMA
     vmem = pl.BlockSpec(memory_space=pltpu.VMEM)
-    return pl.pallas_call(
+    solved = pl.pallas_call(
         kernel,
         out_shape=(
             jax.ShapeDtypeStruct(right_side.shape, jnp.float32),
@@ -652,6 +657,13 @@
         ),
         name="cycle",
     )(col_block, wall_mask, right_side, relax_rate, drift_speed, upwind_sign, blocks)
+    return pl.pallas_call(
+        handed_on,
+        out_shape=tuple(jax.ShapeDtypeStruct(value.shape, value.dtype) for value in solved),
+        in_specs=[vmem, vmem],
+        out_specs=(vmem, vmem),
+        name="handed_on",
+    )(*solved)
 
 
 def solution(mesh):

time: 77.9 us -> 75.2 us (0.965)
  local copies, waits for them, and re-layouts: 3.07 us -> 0 us
    unnamed x2 -> x0, local copies, waits for them, and re-layouts: 3.07 us -> none
    pallas_call x0 -> x1, Pallas kernels: none -> 1.82 us  [per_device(): pl.pallas_call(handed_on, out_shape=tuple((jax.ShapeDtypeStruct(value.sha...]
    pallas_call x1, Pallas kernels: 74 us -> 72.6 us  [per_device(): pl.pallas_call(kernel, out_shape=(jax.ShapeDtypeStruct(right_side.shape,...]
where the time goes in v4:
time: 75.2 us; the launch traced here: 75.1 us
  Pallas kernels  74.4 us (99%)
    pallas_call x1, Pallas kernels, per_device(): pl.pallas_call(kernel, out_shape=(jax.ShapeDtypeStruct(right_side.shape,...  72.6 us
    pallas_call x1, Pallas kernels, per_device(): pl.pallas_call(handed_on, out_shape=tuple((jax.ShapeDtypeStruct(value.sha...  1.82 us

profile of v4, /device:TPU:0, one launch (start us, length us, event | category | flops | bytes accessed | tf_op | source)
XLA Modules:
  0.0 75.1 jit_solution(4102086651620989602)
XLA Ops:
  0.6 72.6 %cycle.1 = (f32[8,8,1792]{2,1,0:T(8,128)}, f32[4,3]{1,0:T(4,128)}) custom-call(s32[14,32]{1,0:T(8,128)} %col_hbm.1, s32[8,8]{1,0:T(8,128)} %wall_hbm.1, f32[8,8,1792]{2,1,0:T(8,128)} %right_hbm.1, f32[1792]{0:T(1024)} %relax_hbm.1, f32[2,1792]{1,0:T(2,128)} %drift_hbm.1, s32[2,1792]{1,0:T(2,128)} %sign_hbm.1, bf16[14,32,128,128]{3,2,1,0:T(8,128)(2,1)} %blocks_ref.1), custom_call_target="tpu_custom_call" | custom-call | tf_op jit(solution)/shard_map/cycle/pallas_call | solution.py:617
  73.2 1.8 %handed_on.1 = (f32[8,8,1792]{2,1,0:T(8,128)}, f32[4,3]{1,0:T(4,128)}) custom-call(f32[8,8,1792]{2,1,0:T(8,128)} %get-tuple-element.4.solution_in, f32[4,3]{1,0:T(4,128)} %get-tuple-element.5.hessenberg_in), custom_call_target="tpu_custom_call" | custom-call | tf_op jit(solution)/shard_map/handed_on/pallas_call | solution.py:660

commit v5 on v4

--- a/solution.py
+++ b/solution.py
@@ -341,8 +341,9 @@
                 device_id_type=MESH,
             )
 
-        following = {("A1", 0): ("A2", "Z"), ("A1", 2): ("A2", "Z"), ("A3", 1): ("A2", "Z"), ("A3", 3): ("A2", "Z")}
+        following = {}
         for q in range(QUARTERS):
+            following["A3" if q % 2 else "A1", q] = ("A2", "Z")
             following["Z0", q] = ("B",)
             following["B", q] = ("C2",)
 
@@ -496,54 +497,55 @@
 
         compute_first((0, 0, 0))
         compute((0, 0, 1))
+        dots_with(j)
         take("A1", 0)
         take("A3", 0)
         take("Z0", 0)
+        take("A1", 1)
         take("A3", 1)
-        take("A1", 1)
-        take("Z0", 1)
-        dots_with(j)
         if j == 0:
             post(0, 1, collect(0, 0))
+        take("Z0", 1)
         take("A1", 2)
         take("A3", 2)
         take("Z0", 2)
+        take("A1", 3)
         take("A3", 3)
-        take("A1", 3)
-        take("Z0", 3)
         start(faces[0])
         compute((0, 1, 0))
+        compute((0, 3, 0))
+        take("Z0", 3)
+        compute((0, 1, 1))
+        take("A2", 0)
         take("B", 0)
-        take("A2", 0)
+        compute((0, 3, 1))
+        compute((1, 0, 0))
         take("A2", 1)
-        compute((0, 3, 0))
         take("B", 1)
-        compute((1, 0, 0))
         take("Z", 0)
-        compute((0, 1, 1))
-        take("B", 2)
-        compute((0, 3, 1))
-        take("B", 3)
-        take("Z", 1)
-        take("A2", 2)
         compute((1, 0, 1))
-        take("A2", 3)
         if j == 0:
             squared, diagonal = unpack(collect(0, 1), 2)
             shift = diagonal / (squared + epsilon)
         local_terms()
+        take("Z", 1)
+        take("A2", 2)
+        take("B", 2)
+        take("A2", 3)
+        take("B", 3)
+        compute((0, 2, 0))
         take("Z", 2)
-        compute((0, 2, 0))
-        take("C2", 0, 1)
+        compute((1, 1, 0))
+        take("C2", 1)
         compute((0, 2, 1))
         take("Z", 3)
-        compute((1, 1, 0))
+        take("C2", 0)
+        compute((1, 1, 1))
+        compute((1, 3, 0))
+        edge_terms()
+        compute((1, 3, 1))
         take("C2", 2)
-        compute((1, 3, 0))
         take("C2", 3)
-        compute((1, 1, 1))
-        compute((1, 3, 1))
-        edge_terms()
         compute((1, 2, 0))
         place = (1, 2, 1)
         ready(place)

time: 75.2 us -> 74.4 us (0.989)
    pallas_call x1, Pallas kernels: 72.6 us -> 71.8 us  [per_device(): pl.pallas_call(kernel, out_shape=(jax.ShapeDtypeStruct(right_side.shape,...]
where the time goes in v5:
time: 74.4 us; the launch traced here: 74.3 us
  Pallas kernels  73.7 us (99%)
    pallas_call x1, Pallas kernels, per_device(): pl.pallas_call(kernel, out_shape=(jax.ShapeDtypeStruct(right_side.shape,...  71.8 us
    pallas_call x1, Pallas kernels, per_device(): pl.pallas_call(handed_on, out_shape=tuple((jax.ShapeDtypeStruct(value.sha...  1.82 us

profile of v5, /device:TPU:0, one launch (start us, length us, event | category | flops | bytes accessed | tf_op | source)
XLA Modules:
  0.0 74.3 jit_solution(1378775670086912573)
XLA Ops:
  0.6 71.8 %cycle.1 = (f32[8,8,1792]{2,1,0:T(8,128)}, f32[4,3]{1,0:T(4,128)}) custom-call(s32[14,32]{1,0:T(8,128)} %col_hbm.1, s32[8,8]{1,0:T(8,128)} %wall_hbm.1, f32[8,8,1792]{2,1,0:T(8,128)} %right_hbm.1, f32[1792]{0:T(1024)} %relax_hbm.1, f32[2,1792]{1,0:T(2,128)} %drift_hbm.1, s32[2,1792]{1,0:T(2,128)} %sign_hbm.1, bf16[14,32,128,128]{3,2,1,0:T(8,128)(2,1)} %blocks_ref.1), custom_call_target="tpu_custom_call" | custom-call | tf_op jit(solution)/shard_map/cycle/pallas_call | solution.py:619
  72.5 1.8 %handed_on.1 = (f32[8,8,1792]{2,1,0:T(8,128)}, f32[4,3]{1,0:T(4,128)}) custom-call(f32[8,8,1792]{2,1,0:T(8,128)} %get-tuple-element.4.solution_in, f32[4,3]{1,0:T(4,128)} %get-tuple-element.5.hessenberg_in), custom_call_target="tpu_custom_call" | custom-call | tf_op jit(solution)/shard_map/handed_on/pallas_call | solution.py:662
